TPU v7x, 256 devices: a whole 4x4x8 slice. The times are simulated.
256 devices in a mesh: seq: 8 (over y, core), chan: 32 (over z, x).
Axes of the slice: x: 4, y: 4, z: 8, core: 2. Of those that a mesh axis runs over, the one named last changes fastest.
Arguments:
- tokens: bfloat16 [1024, 4096], P('seq', 'chan'), may hold values from -6 to 6
- in_weight: bfloat16 [4096, 3, 4096], P(None, None, 'chan'), may hold values from -0.09375 to 0.09375
- short_kernel: float32 [3, 3, 4096], P(None, None, 'chan'), may hold values from -3 to 3
- filters: float32 [2, 1024, 4096], P(None, 'seq', 'chan'), may hold values from -0.5 to 0.5
- skip_gain: float32 [2, 4096], P(None, 'chan'), may hold values from 0.5 to 1.5
- out_weight: bfloat16 [4096, 4096], P('chan'), may hold values from -0.09375 to 0.09375
- cotangent: bfloat16 [1024, 4096], P('seq', 'chan'), may hold values from -6 to 6
Outputs:
- mixed: bfloat16 [1024, 4096], P('seq', 'chan')
- token_grad: bfloat16 [1024, 4096], P('seq', 'chan')
All inputs are finite; a program needn't handle non-finite values.
Results may differ from a plain program's by a relative error of at most 0.0049.
Values may be sent and summed in bfloat16 or wider, within the bound.
No kernel may reach another device: no remote copies, remote signals or barrier semaphores. Data moves between devices by JAX's collectives and lax.ppermute only.
A program may use at most 64 MiB of HBM per device.

v0:
```python
import math
import jax
import jax.numpy as jnp
from jax import lax
from jax.sharding import PartitionSpec as P

PRECISE = lax.Precision.HIGHEST


def swapped(value, axis, apart):
    mask = 2**apart
    pairs = [(source, source ^ mask) for source in range(lax.axis_size(axis))]
    return lax.ppermute(value, axis, pairs)


def passed_along(value, axis, steps):
    count = lax.axis_size(axis)
    first, last = (max(0, -steps), min(count, count - steps))
    return lax.ppermute(value, axis, [(source, source + steps) for source in range(first, last)])


def rotate(real_part, imag_part, turn_angle):
    cosine = jnp.cos(turn_angle)
    sine_part = jnp.sin(turn_angle)
    return (real_part * cosine - imag_part * sine_part, real_part * sine_part + imag_part * cosine)


def block_dft(real_part, imag_part, flip_sign):
    full_shape = real_part.shape
    length = full_shape[-2]
    token_positions = jnp.arange(length, dtype=jnp.int32)
    table_angle = (
        2.0
        * math.pi
        / length
        * (token_positions[:, None] * token_positions[None, :] % length).astype(jnp.float32)
    )
    cosine = jnp.cos(table_angle)
    sine_part = flip_sign * jnp.sin(table_angle)
    summed = cosine + sine_part
    differ = sine_part - cosine
    flat_re = real_part.reshape((-1, length, full_shape[-1]))
    flat_im = imag_part.reshape((-1, length, full_shape[-1]))
    product_one = jnp.einsum("kn,anc->akc", cosine, flat_re + flat_im, precision=PRECISE)
    product_two = jnp.einsum("kn,anc->akc", summed, flat_im, precision=PRECISE)
    product_three = jnp.einsum("kn,anc->akc", differ, flat_re, precision=PRECISE)
    return (
        (product_one - product_two).reshape(full_shape),
        (product_one + product_three).reshape(full_shape),
    )


def twiddle(real_part, imag_part, column, full_length, flip_sign):
    row_ids = jnp.arange(real_part.shape[-2], dtype=jnp.int32)[:, None]
    turn_angle = (
        flip_sign
        * 2.0
        * math.pi
        / full_length
        * (column * row_ids % full_length).astype(jnp.float32)
    )
    return rotate(real_part, imag_part, turn_angle)


def reversed_index(seq_index, levels):
    flipped = jnp.zeros((), jnp.int32)
    for section_bit in range(levels):
        flipped = flipped + seq_index // 2**section_bit % 2 * 2 ** (levels - 1 - section_bit)
    return flipped


def spectrum(signal):
    seq_count = lax.axis_size("seq")
    levels = seq_count.bit_length() - 1
    seq_index = lax.axis_index("seq")
    blocks = signal.shape[1]
    full_length = 2 * seq_count * blocks
    quarter = jnp.arange(2, dtype=jnp.int32)
    lift_angle = -math.pi / seq_count * seq_index.astype(jnp.float32)
    real_part = jnp.stack([signal, signal * jnp.cos(lift_angle)])
    imag_part = jnp.stack([jnp.zeros_like(signal), signal * jnp.sin(lift_angle)])
    for section_bit in reversed(range(levels)):
        half_span = 2**section_bit
        other_re, other_im = swapped((real_part, imag_part), "seq", section_bit)
        is_upper = seq_index // half_span % 2 == 1
        phase_angle = -math.pi / half_span * (seq_index % half_span).astype(jnp.float32)
        diff_re, diff_im = rotate(other_re - real_part, other_im - imag_part, phase_angle)
        real_part = jnp.where(is_upper, diff_re, real_part + other_re)
        imag_part = jnp.where(is_upper, diff_im, imag_part + other_im)
    column = 2 * reversed_index(seq_index, levels) + quarter[:, None, None, None]
    real_part, imag_part = twiddle(real_part, imag_part, column, full_length, -1.0)
    return block_dft(real_part, imag_part, -1.0)


def restore(real_part, imag_part):
    seq_count = lax.axis_size("seq")
    levels = seq_count.bit_length() - 1
    seq_index = lax.axis_index("seq")
    blocks = real_part.shape[-2]
    full_length = 2 * seq_count * blocks
    quarter = jnp.arange(2, dtype=jnp.int32)
    real_part, imag_part = block_dft(real_part, imag_part, 1.0)
    real_part = real_part / blocks
    imag_part = imag_part / blocks
    column = 2 * reversed_index(seq_index, levels) + quarter[:, None, None, None]
    real_part, imag_part = twiddle(real_part, imag_part, column, full_length, 1.0)
    for section_bit in range(levels):
        half_span = 2**section_bit
        other_re, other_im = swapped((real_part, imag_part), "seq", section_bit)
        is_upper = seq_index // half_span % 2 == 1
        phase_angle = math.pi / half_span * (seq_index % half_span).astype(jnp.float32)
        turned_re, turned_im = rotate(other_re, other_im, phase_angle)
        local_rotated_real, own_turn_im = rotate(real_part, imag_part, phase_angle)
        new_re = jnp.where(is_upper, other_re - local_rotated_real, real_part + turned_re)
        new_im = jnp.where(is_upper, other_im - own_turn_im, imag_part + turned_im)
        real_part = 0.5 * new_re
        imag_part = 0.5 * new_im
    lift_angle = math.pi / seq_count * seq_index.astype(jnp.float32)
    return 0.5 * (
        real_part[0] + real_part[1] * jnp.cos(lift_angle) - imag_part[1] * jnp.sin(lift_angle)
    )


def product_of(left_pair, right_pair, conjugate):
    left_re, left_im = left_pair
    right_re, right_im = right_pair
    if conjugate:
        right_im = -right_im
    return (left_re * right_re - left_im * right_im, left_re * right_im + left_im * right_re)


def select_entry(pair, entry):
    return (pair[0][:, entry : entry + 1], pair[1][:, entry : entry + 1])


def on_device(tokens, in_weight, short_kernel, filters, skip_gain, out_weight, cotangent):
    chans = in_weight.shape[2]
    width = in_weight.shape[0]
    blocks = tokens.shape[0]
    flat_in = in_weight.reshape((width, 3 * chans))
    projected = jnp.dot(
        lax.all_gather(tokens, "chan", axis=1, tiled=True),
        flat_in,
        preferred_element_type=jnp.float32,
    )
    projected = projected.reshape((blocks, 3, chans))
    taps = short_kernel.shape[0]
    prior = passed_along(projected[blocks - (taps - 1) :], "seq", 1)
    padded = jnp.concatenate([prior, projected], axis=0)
    shorted = short_kernel[0] * projected
    for tap_index in range(1, taps):
        offset = taps - 1 - tap_index
        shorted = shorted + short_kernel[tap_index] * padded[offset : offset + blocks]
    values = shorted[:, 0]
    gate_one = shorted[:, 1]
    gate_two = shorted[:, 2]
    spectra = spectrum(jnp.stack([filters[0], filters[1], values]))
    conv_one = (
        restore(*product_of(select_entry(spectra, 2), select_entry(spectra, 0), False))[0]
        + skip_gain[0] * values
    )
    first_out = gate_one * conv_one
    first_spec = spectrum(first_out[None])
    conv_two = (
        restore(*product_of(first_spec, select_entry(spectra, 1), False))[0]
        + skip_gain[1] * first_out
    )
    second_order_output = (gate_two * conv_two).astype(jnp.bfloat16)
    picked = out_weight
    mixed = lax.psum_scatter(
        lax.dot_general(
            picked,
            second_order_output,
            (((0,), (1,)), ((), ())),
            preferred_element_type=jnp.float32,
        ),
        "chan",
        scatter_dimension=0,
        tiled=True,
    ).T.astype(jnp.bfloat16)
    grad_two = lax.dot_general(
        lax.all_gather(cotangent, "chan", axis=1, tiled=True),
        out_weight,
        (((1,), (1,)), ((), ())),
        preferred_element_type=jnp.float32,
    )
    grad_gate_two = grad_two * conv_two
    grad_conv_two = grad_two * gate_two
    grad_spec = spectrum(grad_conv_two[None])
    grad_first = (
        restore(*product_of(grad_spec, select_entry(spectra, 1), True))[0]
        + skip_gain[1] * grad_conv_two
    )
    first_gate_gradient = grad_first * conv_one
    grad_conv_one = grad_first * gate_one
    inner_spec = spectrum(grad_conv_one[None])
    grad_values = (
        restore(*product_of(inner_spec, select_entry(spectra, 0), True))[0]
        + skip_gain[0] * grad_conv_one
    )
    grad_short = jnp.stack([grad_values, first_gate_gradient, grad_gate_two], axis=1)
    later = passed_along(grad_short[: taps - 1], "seq", -1)
    padded_grad = jnp.concatenate([grad_short, later], axis=0)
    grad_proj = short_kernel[0] * grad_short
    for tap_index in range(1, taps):
        grad_proj = (
            grad_proj + short_kernel[tap_index] * padded_grad[tap_index : tap_index + blocks]
        )
    grad_proj = grad_proj.astype(jnp.bfloat16)
    grad_flat = grad_proj.reshape((blocks, 3 * chans))
    picked = flat_in
    token_grad = lax.psum_scatter(
        lax.dot_general(
            picked, grad_flat, (((1,), (1,)), ((), ())), preferred_element_type=jnp.float32
        ),
        "chan",
        scatter_dimension=0,
        tiled=True,
    ).T.astype(jnp.bfloat16)
    return (mixed, token_grad)


def solution(mesh):
    in_specs = (
        P("seq", "chan"),
        P(None, None, "chan"),
        P(None, None, "chan"),
        P(None, "seq", "chan"),
        P(None, "chan"),
        P("chan", None),
        P("seq", "chan"),
    )
    out_specs = (P("seq", "chan"), P("seq", "chan"))
    return jax.shard_map(
        on_device, mesh=mesh, in_specs=in_specs, out_specs=out_specs, check_vma=False
    )
```

profile of v0, /device:TPU:8, one launch (start us, length us, event | category | flops | bytes accessed | tf_op | source)
XLA Modules:
  0.0 760.7 jit_solution(1646638522925081413)
XLA Ops:
  8.9 4.8 copy.188
  13.7 70.3 %all-gather.3.cloned.1.call-done = bf16[128,4096]{1,0:T(8,128)(2,1)} async-done(((bf16[128,128]{1,0:T(8,128)(2,1)}), bf16[128,4096]{1,0:T(8,128)(2,1)}) %all-gather.3.cloned.1.call-update) | async-done | bytes 1048592 | tf_op jit(solution)/shard_map/all_gather | solution.py:142
  84.0 3.3 fusion.349
  87.3 1.9 collective-permute-start
  89.3 66.9 %all-gather.5.cloned.1.call-done = bf16[128,4096]{1,0:T(8,128)(2,1)} async-done(((bf16[128,128]{1,0:T(8,128)(2,1)}), bf16[128,4096]{1,0:T(8,128)(2,1)}) %all-gather.5.cloned.1.call-update) | async-done | bytes 1048592 | tf_op jit(solution)/shard_map/all_gather | solution.py:182
  156.2 1.7 fusion.350
  158.3 2.2 collective-permute-start.1
  160.6 1.5 collective-permute-start.2
  162.1 2.2 collective-permute-start.25
  164.3 1.5 collective-permute-start.26
  166.2 13.1 %collective-permute-done.25 = f32[2,1,128,128]{3,2,1,0:T(8,128)S(1)} collective-permute-done((f32[2,1,128,128]{3,2,1,0:T(8,128)S(1)}, f32[2,1,128,128]{3,2,1,0:T(8,128)S(1)}, u32[]{:S(2)}, u32[]{:S(2)}) %collective-permute-start.25) | collective-permute-done | bytes 131104 | tf_op jit(solution)/shard_map/ppermute | solution.py:13
  179.3 2.8 collective-permute-done.26
  182.7 1.5 collective-permute-start.28
  184.2 1.3 add_select_fusion.4
  186.1 1.5 collective-permute-start.4
  188.6 2.8 collective-permute-done.28
  192.1 6.9 collective-permute-done.3
  198.9 4.2 collective-permute-done.4
  213.8 1.4 collective-permute-start.34
  215.7 3.8 collective-permute-done.33
  219.6 2.0 collective-permute-done.34
  222.1 3.3 collective-permute-start.36
  225.3 4.1 collective-permute-done.35
  229.5 1.4 collective-permute-done.36
  232.1 2.7 collective-permute-start.38
  234.7 3.2 collective-permute-done.37
  237.9 1.4 collective-permute-done.38
  239.4 1.2 collective-permute-start.39
  241.8 2.6 collective-permute-done.39
  244.4 1.5 collective-permute-done.40
  255.2 4.3 collective-permute-done.10
  259.5 2.0 collective-permute-done.9
  261.6 2.4 collective-permute-start.11
  265.3 3.9 collective-permute-done.11
  269.1 1.8 collective-permute-done.12
  271.1 2.2 collective-permute-start.13
  273.4 1.5 collective-permute-start.14
  274.9 3.8 collective-permute-done.13
  278.7 1.4 collective-permute-done.14
  280.1 1.2 collective-permute-start.15
  282.9 2.4 collective-permute-done.15
  285.3 1.4 collective-permute-done.16
  294.5 1.2 collective-permute-start.21
  296.7 4.3 collective-permute-done.21
  301.0 2.0 collective-permute-done.22
  303.1 1.9 collective-permute-start.23
  305.1 1.7 collective-permute-start.24
  306.7 4.3 collective-permute-done.23
  311.0 1.4 collective-permute-done.24
  312.6 1.7 convolution_bitcast_fusion.1
  316.1 1.3 collective-permute-start.45
  318.2 4.3 collective-permute-done.45
  322.6 2.2 collective-permute-done.46
  324.8 1.8 collective-permute-start.47
  326.6 1.8 collective-permute-start.48
  328.5 4.3 collective-permute-done.47
  332.7 1.4 collective-permute-done.48
  334.3 1.9 collective-permute-start.49
  336.2 1.3 collective-permute-done.49
  337.5 2.5 convolution_bitcast_fusion
  340.0 191.7 %reduce-scatter.3.cloned.1.call-done = f32[128,128]{0,1:T(8,128)} async-done(((f32[4096,128]{0,1:T(8,128)}), f32[128,128]{0,1:T(8,128)}) %reduce-scatter.3.cloned.1.call-update) | async-done | bytes 65552 | tf_op jit(solution)/shard_map/reduce_scatter | solution.py:170
  531.7 1.5 convert_bitcast_fusion.1
  533.2 219.3 %reduce-scatter.5.cloned.1.call-done = f32[128,128]{0,1:T(8,128)} async-done(((f32[4096,128]{0,1:T(8,128)}), f32[128,128]{0,1:T(8,128)}) %reduce-scatter.5.cloned.1.call-update) | async-done | bytes 65552 | tf_op jit(solution)/shard_map/reduce_scatter | solution.py:212
  752.5 1.5 convert_bitcast_fusion
  (170 shorter events, 42.2 us)
Async XLA Ops:
  7.2 149.0 %copy-start = (bf16[128,4096]{1,0:T(8,128)(2,1)S(1)}, bf16[128,4096]{1,0:T(8,128)(2,1)}, u32[]{:S(2)}) copy-start(bf16[128,4096]{1,0:T(8,128)(2,1)} %param.12) | copy-start | bytes 3145732
  7.2 76.8 %all-gather.3.cloned.1.call-start = ((), (), s32[]{:S(2)}) async-start(), calls=%async_computation.2 | async-start | bytes 1081344 | tf_op jit(solution)/shard_map/all_gather | solution.py:142
  7.9 148.3 %all-gather.5.cloned.1.call-start = ((), (), s32[]{:S(2)}) async-start(), calls=%async_computation.4 | async-start | bytes 1081344 | tf_op jit(solution)/shard_map/all_gather | solution.py:182
  8.7 523.1 %reduce-scatter.3.cloned.1.call-start = ((), (), s32[]{:S(2)}) async-start(), calls=%async_computation.3 | async-start | bytes 2162688 | tf_op jit(solution)/shard_map/reduce_scatter | solution.py:170
  13.7 144.4 %copy-start.3 = (f32[3,128]{1,0:T(4,128)}, f32[3,128]{1,0:T(4,128)S(1)}, u32[]{:S(2)}) copy-start(f32[3,128]{1,0:T(4,128)S(1)} %get-tuple-element.98) | copy-start | bytes 4612
  84.0 74.2 %copy-start.2 = (f32[2,128,128]{2,1,0:T(8,128)S(1)}, f32[2,128,128]{2,1,0:T(8,128)}, u32[]{:S(2)}) copy-start(f32[2,128,128]{2,1,0:T(8,128)} %param.10) | copy-start | bytes 393220
  87.3 70.8 %collective-permute-start = (f32[2,3,128]{2,0,1:T(2,128)S(1)}, f32[2,3,128]{2,0,1:T(2,128)S(1)}, u32[]{:S(2)}, u32[]{:S(2)}) collective-permute-start(f32[2,3,128]{2,0,1:T(2,128)S(1)} %slice_bitcast_fusion.13), channel_id=1, source_target_pairs={{0,32},{32,64},{64,96},{96,128},{128,160},{160,192},{192,224},{1,3... | collective-permute-start | bytes 9224 | tf_op jit(solution)/shard_map/ppermute | solution.py:19
  158.3 25.9 %collective-permute-start.1 = (f32[2,3,128,128]{3,2,1,0:T(8,128)S(1)}, f32[2,3,128,128]{3,2,1,0:T(8,128)}, u32[]{:S(2)}, u32[]{:S(2)}) collective-permute-start(f32[2,3,128,128]{3,2,1,0:T(8,128)S(1)} %pad_maximum_fusion), channel_id=1, source_target_pairs={{0,128},{32,160},{64,192},{96,224},{128,0},{160,32},{192,64},{224,... | collective-permute-start | bytes 1179656 | tf_op jit(solution)/shard_map/ppermute | solution.py:13
  160.6 23.7 %collective-permute-start.2 = (f32[2,3,128,128]{3,2,1,0:T(8,128)S(1)}, f32[2,3,128,128]{3,2,1,0:T(8,128)}, u32[]{:S(2)}, u32[]{:S(2)}) collective-permute-start(f32[2,3,128,128]{3,2,1,0:T(8,128)S(1)} %stack.71), channel_id=1, source_target_pairs={{0,128},{32,160},{64,192},{96,224},{128,0},{160,32},{192,64},{224,... | collective-permute-start | bytes 1179656 | tf_op jit(solution)/shard_map/ppermute | solution.py:13
  162.1 17.2 %collective-permute-start.25 = (f32[2,1,128,128]{3,2,1,0:T(8,128)S(1)}, f32[2,1,128,128]{3,2,1,0:T(8,128)S(1)}, u32[]{:S(2)}, u32[]{:S(2)}) collective-permute-start(f32[2,1,128,128]{3,2,1,0:T(8,128)S(1)} %pad_maximum_fusion.6), channel_id=1, source_target_pairs={{0,128},{32,160},{64,192},{96,224},{128,0},{160,32},{192,64},{224,... | collective-permute-start | bytes 393224 | tf_op jit(solution)/shard_map/ppermute | solution.py:13
  164.3 17.7 %collective-permute-start.26 = (f32[2,1,128,128]{3,2,1,0:T(8,128)S(1)}, f32[2,1,128,128]{3,2,1,0:T(8,128)S(1)}, u32[]{:S(2)}, u32[]{:S(2)}) collective-permute-start(f32[2,1,128,128]{3,2,1,0:T(8,128)S(1)} %stack.77), channel_id=1, source_target_pairs={{0,128},{32,160},{64,192},{96,224},{128,0},{160,32},{192,64},{224,... | collective-permute-start | bytes 393224 | tf_op jit(solution)/shard_map/ppermute | solution.py:13
  182.1 6.5 collective-permute-start.27
  182.7 8.7 %collective-permute-start.28 = (f32[2,1,128,128]{3,2,0,1:T(8,128)S(1)}, f32[2,1,128,128]{3,2,0,1:T(8,128)S(1)}, u32[]{:S(2)}, u32[]{:S(2)}) collective-permute-start(f32[2,1,128,128]{3,2,0,1:T(8,128)S(1)} %get-tuple-element.81), channel_id=1, source_target_pairs={{0,64},{32,96},{64,0},{96,32},{128,192},{160,224},{192,128},{224,1... | collective-permute-start | bytes 393224 | tf_op jit(solution)/shard_map/ppermute | solution.py:13
  185.5 13.4 %collective-permute-start.3 = (f32[2,3,128,128]{3,2,1,0:T(8,128)S(1)}, f32[2,3,128,128]{3,2,1,0:T(8,128)S(1)}, u32[]{:S(2)}, u32[]{:S(2)}) collective-permute-start(f32[2,3,128,128]{3,2,1,0:T(8,128)S(1)} %get-tuple-element.51), channel_id=1, source_target_pairs={{0,64},{32,96},{64,0},{96,32},{128,192},{160,224},{192,128},{224,1... | collective-permute-start | bytes 1179656 | tf_op jit(solution)/shard_map/ppermute | solution.py:13
  186.1 17.0 %collective-permute-start.4 = (f32[2,3,128,128]{3,2,1,0:T(8,128)S(1)}, f32[2,3,128,128]{3,2,1,0:T(8,128)S(1)}, u32[]{:S(2)}, u32[]{:S(2)}) collective-permute-start(f32[2,3,128,128]{3,2,1,0:T(8,128)S(1)} %get-tuple-element.50), channel_id=1, source_target_pairs={{0,64},{32,96},{64,0},{96,32},{128,192},{160,224},{192,128},{224,1... | collective-permute-start | bytes 1179656 | tf_op jit(solution)/shard_map/ppermute | solution.py:13
  187.8 22.9 %copy-start.5 = (f32[2,128]{1,0:T(2,128)}, f32[2,128]{1,0:T(2,128)S(1)}, u32[]{:S(2)}) copy-start(f32[2,128]{1,0:T(2,128)S(1)} %get-tuple-element.103) | copy-start | bytes 3076
  187.8 22.9 %copy-start.7 = (f32[2,128]{1,0:T(2,128)}, f32[2,128]{1,0:T(2,128)S(1)}, u32[]{:S(2)}) copy-start(f32[2,128]{1,0:T(2,128)S(1)} %get-tuple-element.104) | copy-start | bytes 3076
  191.5 12.9 %collective-permute-start.29 = (f32[2,1,128,128]{3,2,0,1:T(8,128)S(1)}, f32[2,1,128,128]{3,2,0,1:T(8,128)S(1)}, u32[]{:S(2)}, u32[]{:S(2)}) collective-permute-start(f32[2,1,128,128]{3,2,0,1:T(8,128)S(1)} %get-tuple-element.78), channel_id=1, source_target_pairs={{0,32},{32,0},{64,96},{96,64},{128,160},{160,128},{192,224},{224,1... | collective-permute-start | bytes 393224 | tf_op jit(solution)/shard_map/ppermute | solution.py:13
  191.6 12.8 %collective-permute-start.30 = (f32[2,1,128,128]{3,2,0,1:T(8,128)S(1)}, f32[2,1,128,128]{3,2,0,1:T(8,128)S(1)}, u32[]{:S(2)}, u32[]{:S(2)}) collective-permute-start(f32[2,1,128,128]{3,2,0,1:T(8,128)S(1)} %get-tuple-element.79), channel_id=1, source_target_pairs={{0,32},{32,0},{64,96},{96,64},{128,160},{160,128},{192,224},{224,1... | collective-permute-start | bytes 393224 | tf_op jit(solution)/shard_map/ppermute | solution.py:13
  203.3 2.3 collective-permute-start.5
  203.4 2.3 collective-permute-start.6
  208.1 17.3 %copy-start.10 = (f32[2,128]{1,0:T(2,128)S(1)}, f32[2,128]{1,0:T(2,128)}, u32[]{:S(2)}) copy-start(f32[2,128]{1,0:T(2,128)} %param.11) | copy-start | bytes 3076
  211.3 1.4 collective-permute-start.31
  211.7 1.3 collective-permute-start.32
  213.1 6.5 collective-permute-start.33
  213.8 7.8 %collective-permute-start.34 = (f32[2,1,128,128]{3,2,1,0:T(8,128)S(1)}, f32[2,1,128,128]{3,2,1,0:T(8,128)S(1)}, u32[]{:S(2)}, u32[]{:S(2)}) collective-permute-start(f32[2,1,128,128]{3,2,1,0:T(8,128)S(1)} %get-tuple-element.74), channel_id=1, source_target_pairs={{0,64},{32,96},{64,0},{96,32},{128,192},{160,224},{192,128},{224,1... | collective-permute-start | bytes 393224 | tf_op jit(solution)/shard_map/ppermute | solution.py:13
  221.7 7.7 %collective-permute-start.35 = (f32[2,1,128,128]{3,2,1,0:T(8,128)S(1)}, f32[2,1,128,128]{3,2,1,0:T(8,128)S(1)}, u32[]{:S(2)}, u32[]{:S(2)}) collective-permute-start(f32[2,1,128,128]{3,2,1,0:T(8,128)S(1)} %get-tuple-element.72), channel_id=1, source_target_pairs={{0,128},{32,160},{64,192},{96,224},{128,0},{160,32},{192,64},{224,... | collective-permute-start | bytes 393224 | tf_op jit(solution)/shard_map/ppermute | solution.py:13
  222.1 8.8 %collective-permute-start.36 = (f32[2,1,128,128]{3,2,1,0:T(8,128)S(1)}, f32[2,1,128,128]{3,2,1,0:T(8,128)S(1)}, u32[]{:S(2)}, u32[]{:S(2)}) collective-permute-start(f32[2,1,128,128]{3,2,1,0:T(8,128)S(1)} %get-tuple-element.17), channel_id=1, source_target_pairs={{0,128},{32,160},{64,192},{96,224},{128,0},{160,32},{192,64},{224,... | collective-permute-start | bytes 393224 | tf_op jit(solution)/shard_map/ppermute | solution.py:13
  231.0 6.9 collective-permute-start.37
  232.1 7.2 collective-permute-start.38
  239.3 11.2 %copy-start.6 = (f32[2,128]{1,0:T(2,128)S(1)}, f32[2,128]{1,0:T(2,128)}, u32[]{:S(2)}) copy-start(f32[2,128]{1,0:T(2,128)} %copy-done.5) | copy-start | bytes 3076
  239.3 11.2 %copy-start.8 = (f32[2,128]{1,0:T(2,128)S(1)}, f32[2,128]{1,0:T(2,128)}, u32[]{:S(2)}) copy-start(f32[2,128]{1,0:T(2,128)} %copy-done.7) | copy-start | bytes 3076
  239.4 5.1 collective-permute-start.39
  240.7 5.2 collective-permute-start.40
  245.9 1.4 collective-permute-start.41
  246.1 1.6 collective-permute-start.42
  251.1 1.4 collective-permute-start.7
  251.6 1.3 collective-permute-start.8
  253.0 6.5 collective-permute-start.10
  254.2 7.3 collective-permute-start.9
  261.6 7.5 collective-permute-start.11
  264.0 6.9 collective-permute-start.12
  271.1 7.5 collective-permute-start.13
  273.4 6.7 collective-permute-start.14
  280.1 5.2 collective-permute-start.15
  281.4 5.3 collective-permute-start.16
  286.7 1.5 collective-permute-start.17
  286.9 1.8 collective-permute-start.18
  292.7 1.4 collective-permute-start.19
  293.1 1.3 collective-permute-start.20
  294.5 6.5 collective-permute-start.21
  295.8 7.3 collective-permute-start.22
  303.1 7.9 %collective-permute-start.23 = (f32[2,1,128,128]{3,2,0,1:T(8,128)S(1)}, f32[2,1,128,128]{3,2,0,1:T(8,128)S(1)}, u32[]{:S(2)}, u32[]{:S(2)}) collective-permute-start(f32[2,1,128,128]{3,2,0,1:T(8,128)S(1)} %get-tuple-element.64), channel_id=1, source_target_pairs={{0,128},{32,160},{64,192},{96,224},{128,0},{160,32},{192,64},{224,... | collective-permute-start | bytes 393224 | tf_op jit(solution)/shard_map/ppermute | solution.py:13
  305.1 7.4 collective-permute-start.24
  314.3 23.2 %copy-start.4 = (f32[3,128]{1,0:T(4,128)S(1)}, f32[3,128]{1,0:T(4,128)}, u32[]{:S(2)}) copy-start(f32[3,128]{1,0:T(4,128)} %copy-done.3) | copy-start | bytes 4612
  314.3 438.1 %reduce-scatter.5.cloned.1.call-start = ((), (), s32[]{:S(2)}) async-start(), calls=%async_computation.5 | async-start | bytes 2162688 | tf_op jit(solution)/shard_map/reduce_scatter | solution.py:212
  314.4 23.2 %copy-start.1 = (bf16[4096,3,128]{2,0,1:T(8,128)(2,1)S(1)}, bf16[4096,3,128]{2,0,1:T(8,128)(2,1)}, u32[]{:S(2)}) copy-start(bf16[4096,3,128]{2,0,1:T(8,128)(2,1)} %param.8) | copy-start | bytes 9437188
  314.4 1.4 collective-permute-start.43
  314.5 1.5 collective-permute-start.44
  316.1 6.5 collective-permute-start.45
  317.4 7.3 collective-permute-start.46
  324.8 7.9 %collective-permute-start.47 = (f32[2,1,128,128]{3,2,1,0:T(8,128)S(1)}, f32[2,1,128,128]{3,2,1,0:T(8,128)S(1)}, u32[]{:S(2)}, u32[]{:S(2)}) collective-permute-start(f32[2,1,128,128]{3,2,1,0:T(8,128)S(1)} %broadcast_multiply_fusion.4), channel_id=1, source_target_pairs={{0,128},{32,160},{64,192},{96,224},{128,0},{160,32},{192,64},{224,... | collective-permute-start | bytes 393224 | tf_op jit(solution)/shard_map/ppermute | solution.py:13
  326.6 7.5 collective-permute-start.48
  334.3 3.2 collective-permute-start.49
  (1 other events, 4.9 us)
Sparse Core Ops, SparseCore 0:
  10.4 73.5 all-gather.2
  86.5 69.6 all-gather.4
  314.5 217.2 reduce-scatter.2
  535.4 217.0 reduce-scatter.4
where the time goes:
time: 768 us; the launch traced here: 761 us
  waiting for transfers between devices  653 us (85%)
  starting transfers between devices  56.1 us (7%)
  matrix products  23.4 us (3%)
  between operations  15.8 us (2%)
    reduce_scatter x1, waiting for transfers between devices, on_device(): lax.psum_scatter(lax.dot_general(picked, grad_flat, (((1,), (1,)), ((), (...  219 us
    reduce_scatter x1, waiting for transfers between devices, on_device(): lax.psum_scatter(lax.dot_general(picked, second_order_output, (((0,), (1,...  192 us
    ppermute x48, waiting for transfers between devices, swapped(): return lax.ppermute(value, axis, pairs)  102 us
    all_gather x1, waiting for transfers between devices, on_device(): lax.all_gather(tokens, 'chan', axis=1, tiled=True)  70.3 us
    all_gather x1, waiting for transfers between devices, on_device(): lax.all_gather(cotangent, 'chan', axis=1, tiled=True)  66.9 us
    ppermute x48, starting transfers between devices, swapped(): return lax.ppermute(value, axis, pairs)  52.1 us
  transfers between devices with their start and end apart: 54, of which 47 were waited for; matrix products, arithmetic and copies ran while one was open for 2% of the time, Pallas kernels for 0%

commit v1 on v0

--- a/solution.py
+++ b/solution.py
@@ -178,8 +178,14 @@
         scatter_dimension=0,
         tiled=True,
     ).T.astype(jnp.bfloat16)
+    slabs_render = lambda z_in: jnp.concatenate(
+        jax.lax.all_to_all(
+            jnp.stack([z_in for _ in range(jax.lax.axis_size("chan"))], 0), "chan", 0, 0
+        ),
+        axis=1,
+    )
     grad_two = lax.dot_general(
-        lax.all_gather(cotangent, "chan", axis=1, tiled=True),
+        slabs_render(cotangent),
         out_weight,
         (((1,), (1,)), ((), ())),
         preferred_element_type=jnp.float32,

time: 768 us -> 711 us (0.926)
  waiting for transfers between devices: 653 us -> 582 us
  starting transfers between devices: 56.1 us -> 67.4 us
    all_gather x1 -> x0, waiting for transfers between devices: 66.9 us -> none  [on_device(): lax.all_gather(cotangent, 'chan', axis=1, tiled=True)]
    all_to_all x0 -> x1, starting transfers between devices: none -> 11.3 us  [on_device(): jax.lax.all_to_all(jnp.stack([z_in for _ in range(jax.lax.axis_size('chan...]
    all_gather x1, waiting for transfers between devices: 70.3 us -> 60 us  [on_device(): lax.all_gather(tokens, 'chan', axis=1, tiled=True)]
  transfers between devices with their start and end apart: 54 -> 54, of which waited for: 47 -> 47; matrix products, arithmetic and copies ran while one was open for 2% -> 3% of each run, Pallas kernels for 0% -> 0%
where the time goes in v1:
time: 711 us; the launch traced here: 703 us
  waiting for transfers between devices  582 us (82%)
  starting transfers between devices  67.4 us (9%)
  matrix products  22.9 us (3%)
  between operations  15.7 us (2%)
  local copies, waits for them, and re-layouts  7.73 us (1%)
  other arithmetic  7.43 us (1%)
    reduce_scatter x1, waiting for transfers between devices, on_device(): lax.psum_scatter(lax.dot_general(picked, grad_flat, (((1,), (1,)), ((), (...  219 us
    reduce_scatter x1, waiting for transfers between devices, on_device(): lax.psum_scatter(lax.dot_general(picked, second_order_output, (((0,), (1,...  192 us
    ppermute x48, waiting for transfers between devices, swapped(): return lax.ppermute(value, axis, pairs)  106 us
    all_gather x1, waiting for transfers between devices, on_device(): lax.all_gather(tokens, 'chan', axis=1, tiled=True)  60 us
    ppermute x48, starting transfers between devices, swapped(): return lax.ppermute(value, axis, pairs)  52.1 us
  transfers between devices with their start and end apart: 54, of which 47 were waited for; matrix products, arithmetic and copies ran while one was open for 3% of the time, Pallas kernels for 0%

profile of v1, /device:TPU:8, one launch (start us, length us, event | category | flops | bytes accessed | tf_op | source)
XLA Modules:
  0.0 702.9 jit_solution(2248353483719122339)
XLA Ops:
  10.0 11.3 %all-to-all-start = ((bf16[32,128,128]{1,2,0:T(8,128)(2,1)}), bf16[32,128,128]{1,2,0:T(8,128)(2,1)S(1)}, u32[]{:S(2)}, u32[]{:S(2)}) async-start(bf16[32,128,128]{1,2,0:T(8,128)(2,1)} %stack.54), calls=%async_computation.1 | async-start | bytes 2097152 | tf_op jit(solution)/shard_map/all_to_all | solution.py:182
  21.6 4.8 copy.188
  26.4 60.0 %all-gather.2.cloned.1.call-done = bf16[128,4096]{1,0:T(8,128)(2,1)} async-done(((bf16[128,128]{1,0:T(8,128)(2,1)}), bf16[128,4096]{1,0:T(8,128)(2,1)}) %all-gather.2.cloned.1.call-update) | async-done | bytes 1048592 | tf_op jit(solution)/shard_map/all_gather | solution.py:142
  86.4 3.3 fusion.349
  89.7 1.9 collective-permute-start
  92.4 2.2 collective-permute-done
  94.8 2.2 collective-permute-start.1
  97.1 1.5 collective-permute-start.2
  98.6 2.2 collective-permute-start.25
  100.8 1.5 collective-permute-start.26
  102.7 16.8 %collective-permute-done.25 = f32[2,1,128,128]{3,2,1,0:T(8,128)S(1)} collective-permute-done((f32[2,1,128,128]{3,2,1,0:T(8,128)S(1)}, f32[2,1,128,128]{3,2,1,0:T(8,128)S(1)}, u32[]{:S(2)}, u32[]{:S(2)}) %collective-permute-start.25) | collective-permute-done | bytes 131104 | tf_op jit(solution)/shard_map/ppermute | solution.py:13
  119.5 1.4 collective-permute-done.26
  121.6 1.5 collective-permute-start.28
  123.0 1.3 add_select_fusion.4
  125.0 1.5 collective-permute-start.4
  127.4 2.8 collective-permute-done.28
  130.8 7.8 %collective-permute-done.3 = f32[2,3,128,128]{3,2,1,0:T(8,128)S(1)} collective-permute-done((f32[2,3,128,128]{3,2,1,0:T(8,128)S(1)}, f32[2,3,128,128]{3,2,1,0:T(8,128)S(1)}, u32[]{:S(2)}, u32[]{:S(2)}) %collective-permute-start.3) | collective-permute-done | bytes 393248 | tf_op jit(solution)/shard_map/ppermute | solution.py:13
  138.6 6.0 collective-permute-done.4
  157.9 3.8 collective-permute-done.33
  161.7 2.0 collective-permute-done.34
  164.6 2.9 collective-permute-start.36
  167.5 4.1 collective-permute-done.35
  171.6 1.4 collective-permute-done.36
  174.2 2.7 collective-permute-start.38
  176.9 3.2 collective-permute-done.37
  180.0 1.4 collective-permute-done.38
  181.5 1.6 collective-permute-start.39
  183.9 2.6 collective-permute-done.39
  186.5 1.8 collective-permute-done.40
  197.6 4.3 collective-permute-done.10
  201.9 2.0 collective-permute-done.9
  204.0 2.1 collective-permute-start.11
  206.1 1.5 collective-permute-start.12
  207.7 4.2 collective-permute-done.11
  211.9 1.5 collective-permute-done.12
  213.6 1.8 collective-permute-start.13
  215.5 1.9 collective-permute-start.14
  217.3 3.5 collective-permute-done.13
  220.8 1.4 collective-permute-done.14
  222.2 1.3 collective-permute-start.15
  225.0 2.3 collective-permute-done.15
  227.3 1.4 collective-permute-done.16
  236.5 1.3 collective-permute-start.21
  238.7 4.3 collective-permute-done.21
  243.0 2.0 collective-permute-done.22
  245.1 2.0 collective-permute-start.23
  247.2 1.6 collective-permute-start.24
  248.7 4.3 collective-permute-done.23
  253.1 1.4 collective-permute-done.24
  254.7 1.7 convolution_bitcast_fusion.1
  258.2 1.3 collective-permute-start.45
  260.3 4.3 collective-permute-done.45
  264.6 2.2 collective-permute-done.46
  266.9 1.8 collective-permute-start.47
  268.7 1.8 collective-permute-start.48
  270.5 4.3 collective-permute-done.47
  274.8 1.4 collective-permute-done.48
  276.4 1.9 collective-permute-start.49
  278.3 1.3 collective-permute-done.49
  279.6 2.5 convolution_bitcast_fusion
  282.1 191.7 %reduce-scatter.3.cloned.1.call-done = f32[128,128]{0,1:T(8,128)} async-done(((f32[4096,128]{0,1:T(8,128)}), f32[128,128]{0,1:T(8,128)}) %reduce-scatter.3.cloned.1.call-update) | async-done | bytes 65552 | tf_op jit(solution)/shard_map/reduce_scatter | solution.py:170
  473.8 1.5 convert_bitcast_fusion.1
  475.2 219.4 %reduce-scatter.5.cloned.1.call-done = f32[128,128]{0,1:T(8,128)} async-done(((f32[4096,128]{0,1:T(8,128)}), f32[128,128]{0,1:T(8,128)}) %reduce-scatter.5.cloned.1.call-update) | async-done | bytes 65552 | tf_op jit(solution)/shard_map/reduce_scatter | solution.py:218
  694.7 1.5 convert_bitcast_fusion
  (168 shorter events, 44.8 us)
Async XLA Ops:
  7.2 84.5 %copy-start = (bf16[128,4096]{1,0:T(8,128)(2,1)S(1)}, bf16[128,4096]{1,0:T(8,128)(2,1)}, u32[]{:S(2)}) copy-start(bf16[128,4096]{1,0:T(8,128)(2,1)} %param.12) | copy-start | bytes 3145732
  7.2 79.2 %all-gather.2.cloned.1.call-start = ((), (), s32[]{:S(2)}) async-start(), calls=%async_computation.3 | async-start | bytes 1081344 | tf_op jit(solution)/shard_map/all_gather | solution.py:142
  10.0 81.6 %all-to-all-start = ((bf16[32,128,128]{1,2,0:T(8,128)(2,1)}), bf16[32,128,128]{1,2,0:T(8,128)(2,1)S(1)}, u32[]{:S(2)}, u32[]{:S(2)}) async-start(bf16[32,128,128]{1,2,0:T(8,128)(2,1)} %stack.54), calls=%async_computation.1 | async-start | bytes 2097152 | tf_op jit(solution)/shard_map/all_to_all | solution.py:182
  21.4 452.4 %reduce-scatter.3.cloned.1.call-start = ((), (), s32[]{:S(2)}) async-start(), calls=%async_computation.4 | async-start | bytes 2162688 | tf_op jit(solution)/shard_map/reduce_scatter | solution.py:170
  21.6 4.8 copy-start.7
  26.4 68.2 %copy-start.3 = (f32[3,128]{1,0:T(4,128)}, f32[3,128]{1,0:T(4,128)S(1)}, u32[]{:S(2)}) copy-start(f32[3,128]{1,0:T(4,128)S(1)} %get-tuple-element.98) | copy-start | bytes 4612
  86.4 8.3 %copy-start.2 = (f32[2,128,128]{2,1,0:T(8,128)S(1)}, f32[2,128,128]{2,1,0:T(8,128)}, u32[]{:S(2)}) copy-start(f32[2,128,128]{2,1,0:T(8,128)} %param.10) | copy-start | bytes 393220
  89.7 4.9 collective-permute-start
  94.8 28.2 %collective-permute-start.1 = (f32[2,3,128,128]{3,2,1,0:T(8,128)S(1)}, f32[2,3,128,128]{3,2,1,0:T(8,128)}, u32[]{:S(2)}, u32[]{:S(2)}) collective-permute-start(f32[2,3,128,128]{3,2,1,0:T(8,128)S(1)} %pad_maximum_fusion), channel_id=1, source_target_pairs={{0,128},{32,160},{64,192},{96,224},{128,0},{160,32},{192,64},{224,... | collective-permute-start | bytes 1179656 | tf_op jit(solution)/shard_map/ppermute | solution.py:13
  97.1 26.0 %collective-permute-start.2 = (f32[2,3,128,128]{3,2,1,0:T(8,128)S(1)}, f32[2,3,128,128]{3,2,1,0:T(8,128)}, u32[]{:S(2)}, u32[]{:S(2)}) collective-permute-start(f32[2,3,128,128]{3,2,1,0:T(8,128)S(1)} %stack.51), channel_id=1, source_target_pairs={{0,128},{32,160},{64,192},{96,224},{128,0},{160,32},{192,64},{224,... | collective-permute-start | bytes 1179656 | tf_op jit(solution)/shard_map/ppermute | solution.py:13
  98.6 20.8 %collective-permute-start.25 = (f32[2,1,128,128]{3,2,1,0:T(8,128)S(1)}, f32[2,1,128,128]{3,2,1,0:T(8,128)S(1)}, u32[]{:S(2)}, u32[]{:S(2)}) collective-permute-start(f32[2,1,128,128]{3,2,1,0:T(8,128)S(1)} %pad_maximum_fusion.6), channel_id=1, source_target_pairs={{0,128},{32,160},{64,192},{96,224},{128,0},{160,32},{192,64},{224,... | collective-permute-start | bytes 393224 | tf_op jit(solution)/shard_map/ppermute | solution.py:13
  100.8 20.0 %collective-permute-start.26 = (f32[2,1,128,128]{3,2,1,0:T(8,128)S(1)}, f32[2,1,128,128]{3,2,1,0:T(8,128)S(1)}, u32[]{:S(2)}, u32[]{:S(2)}) collective-permute-start(f32[2,1,128,128]{3,2,1,0:T(8,128)S(1)} %stack.113), channel_id=1, source_target_pairs={{0,128},{32,160},{64,192},{96,224},{128,0},{160,32},{192,64},{224,... | collective-permute-start | bytes 393224 | tf_op jit(solution)/shard_map/ppermute | solution.py:13
  120.9 6.5 collective-permute-start.27
  121.6 8.6 %collective-permute-start.28 = (f32[2,1,128,128]{3,2,0,1:T(8,128)S(1)}, f32[2,1,128,128]{3,2,0,1:T(8,128)S(1)}, u32[]{:S(2)}, u32[]{:S(2)}) collective-permute-start(f32[2,1,128,128]{3,2,0,1:T(8,128)S(1)} %get-tuple-element.81), channel_id=1, source_target_pairs={{0,64},{32,96},{64,0},{96,32},{128,192},{160,224},{192,128},{224,1... | collective-permute-start | bytes 393224 | tf_op jit(solution)/shard_map/ppermute | solution.py:13
  124.3 14.3 %collective-permute-start.3 = (f32[2,3,128,128]{3,2,1,0:T(8,128)S(1)}, f32[2,3,128,128]{3,2,1,0:T(8,128)S(1)}, u32[]{:S(2)}, u32[]{:S(2)}) collective-permute-start(f32[2,3,128,128]{3,2,1,0:T(8,128)S(1)} %get-tuple-element.51), channel_id=1, source_target_pairs={{0,64},{32,96},{64,0},{96,32},{128,192},{160,224},{192,128},{224,1... | collective-permute-start | bytes 1179656 | tf_op jit(solution)/shard_map/ppermute | solution.py:13
  125.0 19.7 %collective-permute-start.4 = (f32[2,3,128,128]{3,2,1,0:T(8,128)S(1)}, f32[2,3,128,128]{3,2,1,0:T(8,128)S(1)}, u32[]{:S(2)}, u32[]{:S(2)}) collective-permute-start(f32[2,3,128,128]{3,2,1,0:T(8,128)S(1)} %get-tuple-element.50), channel_id=1, source_target_pairs={{0,64},{32,96},{64,0},{96,32},{128,192},{160,224},{192,128},{224,1... | collective-permute-start | bytes 1179656 | tf_op jit(solution)/shard_map/ppermute | solution.py:13
  130.3 15.6 %collective-permute-start.29 = (f32[2,1,128,128]{3,2,0,1:T(8,128)S(1)}, f32[2,1,128,128]{3,2,0,1:T(8,128)S(1)}, u32[]{:S(2)}, u32[]{:S(2)}) collective-permute-start(f32[2,1,128,128]{3,2,0,1:T(8,128)S(1)} %get-tuple-element.78), channel_id=1, source_target_pairs={{0,32},{32,0},{64,96},{96,64},{128,160},{160,128},{192,224},{224,1... | collective-permute-start | bytes 393224 | tf_op jit(solution)/shard_map/ppermute | solution.py:13
  130.4 15.5 %collective-permute-start.30 = (f32[2,1,128,128]{3,2,0,1:T(8,128)S(1)}, f32[2,1,128,128]{3,2,0,1:T(8,128)S(1)}, u32[]{:S(2)}, u32[]{:S(2)}) collective-permute-start(f32[2,1,128,128]{3,2,0,1:T(8,128)S(1)} %get-tuple-element.79), channel_id=1, source_target_pairs={{0,32},{32,0},{64,96},{96,64},{128,160},{160,128},{192,224},{224,1... | collective-permute-start | bytes 393224 | tf_op jit(solution)/shard_map/ppermute | solution.py:13
  144.8 2.3 collective-permute-start.5
  144.9 2.3 collective-permute-start.6
  149.5 18.0 %copy-start.8 = (f32[2,128]{1,0:T(2,128)S(1)}, f32[2,128]{1,0:T(2,128)}, u32[]{:S(2)}) copy-start(f32[2,128]{1,0:T(2,128)} %param.11) | copy-start | bytes 3076
  153.4 1.4 collective-permute-start.31
  153.8 1.3 collective-permute-start.32
  155.3 6.5 collective-permute-start.33
  156.4 7.3 %collective-permute-start.34 = (f32[2,1,128,128]{3,2,1,0:T(8,128)S(1)}, f32[2,1,128,128]{3,2,1,0:T(8,128)S(1)}, u32[]{:S(2)}, u32[]{:S(2)}) collective-permute-start(f32[2,1,128,128]{3,2,1,0:T(8,128)S(1)} %get-tuple-element.74), channel_id=1, source_target_pairs={{0,64},{32,96},{64,0},{96,32},{128,192},{160,224},{192,128},{224,1... | collective-permute-start | bytes 393224 | tf_op jit(solution)/shard_map/ppermute | solution.py:13
  163.8 7.7 %collective-permute-start.35 = (f32[2,1,128,128]{3,2,1,0:T(8,128)S(1)}, f32[2,1,128,128]{3,2,1,0:T(8,128)S(1)}, u32[]{:S(2)}, u32[]{:S(2)}) collective-permute-start(f32[2,1,128,128]{3,2,1,0:T(8,128)S(1)} %get-tuple-element.72), channel_id=1, source_target_pairs={{0,128},{32,160},{64,192},{96,224},{128,0},{160,32},{192,64},{224,... | collective-permute-start | bytes 393224 | tf_op jit(solution)/shard_map/ppermute | solution.py:13
  164.6 8.4 %collective-permute-start.36 = (f32[2,1,128,128]{3,2,1,0:T(8,128)S(1)}, f32[2,1,128,128]{3,2,1,0:T(8,128)S(1)}, u32[]{:S(2)}, u32[]{:S(2)}) collective-permute-start(f32[2,1,128,128]{3,2,1,0:T(8,128)S(1)} %get-tuple-element.17), channel_id=1, source_target_pairs={{0,128},{32,160},{64,192},{96,224},{128,0},{160,32},{192,64},{224,... | collective-permute-start | bytes 393224 | tf_op jit(solution)/shard_map/ppermute | solution.py:13
  173.1 6.9 collective-permute-start.37
  174.2 7.2 %collective-permute-start.38 = (f32[2,1,128,128]{3,2,0,1:T(8,128)S(1)}, f32[2,1,128,128]{3,2,0,1:T(8,128)S(1)}, u32[]{:S(2)}, u32[]{:S(2)}) collective-permute-start(f32[2,1,128,128]{3,2,0,1:T(8,128)S(1)} %pad_bitcast_fusion), channel_id=1, source_target_pairs={{0,128},{32,160},{64,192},{96,224},{128,0},{160,32},{192,64},{224,... | collective-permute-start | bytes 393224 | tf_op jit(solution)/shard_map/ppermute | solution.py:13
  181.5 11.6 %copy-start.5 = (f32[2,128]{1,0:T(2,128)S(1)}, f32[2,128]{1,0:T(2,128)}, u32[]{:S(2)}) copy-start(f32[2,128]{1,0:T(2,128)} %get-tuple-element.103) | copy-start | bytes 3076
  181.5 11.6 %copy-start.6 = (f32[2,128]{1,0:T(2,128)S(1)}, f32[2,128]{1,0:T(2,128)}, u32[]{:S(2)}) copy-start(f32[2,128]{1,0:T(2,128)} %get-tuple-element.104) | copy-start | bytes 3076
  181.5 5.1 collective-permute-start.39
  183.1 5.2 collective-permute-start.40
  188.4 1.4 collective-permute-start.41
  188.5 1.6 collective-permute-start.42
  193.6 1.4 collective-permute-start.7
  194.0 1.3 collective-permute-start.8
  195.5 6.5 collective-permute-start.10
  196.6 7.3 %collective-permute-start.9 = (f32[2,1,128,128]{3,2,0,1:T(8,128)S(1)}, f32[2,1,128,128]{3,2,0,1:T(8,128)S(1)}, u32[]{:S(2)}, u32[]{:S(2)}) collective-permute-start(f32[2,1,128,128]{3,2,0,1:T(8,128)S(1)} %get-tuple-element.41), channel_id=1, source_target_pairs={{0,64},{32,96},{64,0},{96,32},{128,192},{160,224},{192,128},{224,1... | collective-permute-start | bytes 393224 | tf_op jit(solution)/shard_map/ppermute | solution.py:13
  204.0 7.9 %collective-permute-start.11 = (f32[2,1,128,128]{3,2,0,1:T(8,128)S(1)}, f32[2,1,128,128]{3,2,0,1:T(8,128)S(1)}, u32[]{:S(2)}, u32[]{:S(2)}) collective-permute-start(f32[2,1,128,128]{3,2,0,1:T(8,128)S(1)} %get-tuple-element.68), channel_id=1, source_target_pairs={{0,128},{32,160},{64,192},{96,224},{128,0},{160,32},{192,64},{224,... | collective-permute-start | bytes 393224 | tf_op jit(solution)/shard_map/ppermute | solution.py:13
  206.1 7.3 %collective-permute-start.12 = (f32[2,1,128,128]{3,2,0,1:T(8,128)S(1)}, f32[2,1,128,128]{3,2,0,1:T(8,128)S(1)}, u32[]{:S(2)}, u32[]{:S(2)}) collective-permute-start(f32[2,1,128,128]{3,2,0,1:T(8,128)S(1)} %get-tuple-element.39), channel_id=1, source_target_pairs={{0,128},{32,160},{64,192},{96,224},{128,0},{160,32},{192,64},{224,... | collective-permute-start | bytes 393224 | tf_op jit(solution)/shard_map/ppermute | solution.py:13
  213.6 7.2 %collective-permute-start.13 = (f32[2,1,128,128]{3,2,0,1:T(8,128)S(1)}, f32[2,1,128,128]{3,2,0,1:T(8,128)S(1)}, u32[]{:S(2)}, u32[]{:S(2)}) collective-permute-start(f32[2,1,128,128]{3,2,0,1:T(8,128)S(1)} %pad_maximum_fusion.5), channel_id=1, source_target_pairs={{0,128},{32,160},{64,192},{96,224},{128,0},{160,32},{192,64},{224,... | collective-permute-start | bytes 393224 | tf_op jit(solution)/shard_map/ppermute | solution.py:13
  215.5 6.7 collective-permute-start.14
  222.2 5.1 collective-permute-start.15
  223.6 5.1 collective-permute-start.16
  228.7 1.5 collective-permute-start.17
  228.9 1.8 collective-permute-start.18
  234.7 1.4 collective-permute-start.19
  235.1 1.3 collective-permute-start.20
  236.5 6.5 collective-permute-start.21
  237.9 7.1 %collective-permute-start.22 = (f32[2,1,128,128]{3,2,0,1:T(8,128)S(1)}, f32[2,1,128,128]{3,2,0,1:T(8,128)S(1)}, u32[]{:S(2)}, u32[]{:S(2)}) collective-permute-start(f32[2,1,128,128]{3,2,0,1:T(8,128)S(1)} %get-tuple-element.66), channel_id=1, source_target_pairs={{0,64},{32,96},{64,0},{96,32},{128,192},{160,224},{192,128},{224,1... | collective-permute-start | bytes 393224 | tf_op jit(solution)/shard_map/ppermute | solution.py:13
  245.1 7.9 %collective-permute-start.23 = (f32[2,1,128,128]{3,2,0,1:T(8,128)S(1)}, f32[2,1,128,128]{3,2,0,1:T(8,128)S(1)}, u32[]{:S(2)}, u32[]{:S(2)}) collective-permute-start(f32[2,1,128,128]{3,2,0,1:T(8,128)S(1)} %get-tuple-element.64), channel_id=1, source_target_pairs={{0,128},{32,160},{64,192},{96,224},{128,0},{160,32},{192,64},{224,... | collective-permute-start | bytes 393224 | tf_op jit(solution)/shard_map/ppermute | solution.py:13
  247.2 7.3 %collective-permute-start.24 = (f32[2,1,128,128]{3,2,0,1:T(8,128)S(1)}, f32[2,1,128,128]{3,2,0,1:T(8,128)S(1)}, u32[]{:S(2)}, u32[]{:S(2)}) collective-permute-start(f32[2,1,128,128]{3,2,0,1:T(8,128)S(1)} %get-tuple-element.29), channel_id=1, source_target_pairs={{0,128},{32,160},{64,192},{96,224},{128,0},{160,32},{192,64},{224,... | collective-permute-start | bytes 393224 | tf_op jit(solution)/shard_map/ppermute | solution.py:13
  256.4 23.2 %copy-start.4 = (f32[3,128]{1,0:T(4,128)S(1)}, f32[3,128]{1,0:T(4,128)}, u32[]{:S(2)}) copy-start(f32[3,128]{1,0:T(4,128)} %copy-done.3) | copy-start | bytes 4612
  256.4 438.2 %reduce-scatter.5.cloned.1.call-start = ((), (), s32[]{:S(2)}) async-start(), calls=%async_computation.5 | async-start | bytes 2162688 | tf_op jit(solution)/shard_map/reduce_scatter | solution.py:218
  256.5 23.2 %copy-start.1 = (bf16[4096,3,128]{2,0,1:T(8,128)(2,1)S(1)}, bf16[4096,3,128]{2,0,1:T(8,128)(2,1)}, u32[]{:S(2)}) copy-start(bf16[4096,3,128]{2,0,1:T(8,128)(2,1)} %param.8) | copy-start | bytes 9437188
  256.5 1.4 collective-permute-start.43
  256.6 1.5 collective-permute-start.44
  258.2 6.5 collective-permute-start.45
  259.5 7.3 %collective-permute-start.46 = (f32[2,1,128,128]{3,2,1,0:T(8,128)S(1)}, f32[2,1,128,128]{3,2,1,0:T(8,128)S(1)}, u32[]{:S(2)}, u32[]{:S(2)}) collective-permute-start(f32[2,1,128,128]{3,2,1,0:T(8,128)S(1)} %get-tuple-element.62), channel_id=1, source_target_pairs={{0,64},{32,96},{64,0},{96,32},{128,192},{160,224},{192,128},{224,1... | collective-permute-start | bytes 393224 | tf_op jit(solution)/shard_map/ppermute | solution.py:13
  266.9 7.9 %collective-permute-start.47 = (f32[2,1,128,128]{3,2,1,0:T(8,128)S(1)}, f32[2,1,128,128]{3,2,1,0:T(8,128)S(1)}, u32[]{:S(2)}, u32[]{:S(2)}) collective-permute-start(f32[2,1,128,128]{3,2,1,0:T(8,128)S(1)} %broadcast_multiply_fusion.4), channel_id=1, source_target_pairs={{0,128},{32,160},{64,192},{96,224},{128,0},{160,32},{192,64},{224,... | collective-permute-start | bytes 393224 | tf_op jit(solution)/shard_map/ppermute | solution.py:13
  268.7 7.5 %collective-permute-start.48 = (f32[2,1,128,128]{3,2,1,0:T(8,128)S(1)}, f32[2,1,128,128]{3,2,1,0:T(8,128)S(1)}, u32[]{:S(2)}, u32[]{:S(2)}) collective-permute-start(f32[2,1,128,128]{3,2,1,0:T(8,128)S(1)} %get-tuple-element.60), channel_id=1, source_target_pairs={{0,128},{32,160},{64,192},{96,224},{128,0},{160,32},{192,64},{224,... | collective-permute-start | bytes 393224 | tf_op jit(solution)/shard_map/ppermute | solution.py:13
  276.4 3.2 collective-permute-start.49
Sparse Core Ops, SparseCore 0:
  10.4 75.9 all-gather.1
  256.5 217.2 reduce-scatter.2
  477.6 216.9 reduce-scatter.4
